TPU v7x, 32 devices: a whole 2x2x4 slice. The times are simulated.
32 devices in a mesh: aux: 8 (over z, core), orb: 2 (over y), rep: 2 (over x).
Axes of the slice: x: 2, y: 2, z: 4, core: 2. Of those that a mesh axis runs over, the one named last changes fastest.
Arguments:
- slab: bfloat16 [4096, 4, 1024], P('aux', None, 'orb'), may hold values from -6 to 6
- occ_density: bfloat16 [1024, 512], P('orb'), may hold values from -0.25 to 0.25
- virt_density: bfloat16 [1024, 512], P('orb'), may hold values from -0.25 to 0.25
- block_mask: int32 [32, 8], P('aux', 'orb'), may hold values 0 or 1
- matching: int32 [2, 8], replicated, may hold values from 0 to 7, as said below
Outputs:
- chi_pair: float32 [2, 4096, 512], P('rep', ('aux', 'orb'))
- chi_self: float32 [4096, 512], P(('aux', 'orb'), 'rep')
Inputs may be any that keep to these rules, and one draw needn't show every extreme that they name: `matching`: each row pairs the 8 owners: entry p names the partner of p, the partner's entry names p, and no owner is its own partner.
All inputs are finite; a program needn't handle non-finite values. No bound on the sum of `block_mask` on one device may be relied on, other than what follows from the above.
Results may differ from a plain program's by a relative error of at most 0.0041.
Values may be sent and summed in bfloat16 or wider, within the bound.
A program may use at most 64 MiB of HBM per device.

v0:
```python
import math

import jax
import jax.numpy as jnp
from jax import lax
from jax.sharding import PartitionSpec as P

BLOCK = 128


def per_device(slab, occ_density, virt_density, block_mask, matching):
    owners = lax.axis_size("aux")
    rep_index = lax.axis_index("rep")
    aux_rows, batch_rows, orb_cols = slab.shape
    weights = block_mask.astype(jnp.bfloat16)
    spread = jnp.repeat(jnp.repeat(weights, BLOCK, axis=0), BLOCK, axis=1)
    masked = slab * spread[:, None, :]
    occupied = jnp.einsum(
        "plu,ut->plt", masked, occ_density, preferred_element_type=jnp.float32
    ).astype(jnp.bfloat16)
    virtual = jnp.einsum(
        "plu,ut->plt", masked, virt_density, preferred_element_type=jnp.float32
    ).astype(jnp.bfloat16)
    partner = lax.dynamic_index_in_dim(matching, rep_index, 0, keepdims=False)
    pieces = virtual.reshape(owners, aux_rows // owners, batch_rows, orb_cols)
    reordered = jnp.take(
        lax.all_to_all(pieces, "aux", split_axis=0, concat_axis=0, tiled=True), partner, axis=0
    )
    arrived = lax.all_to_all(reordered, "aux", split_axis=0, concat_axis=0, tiled=True)
    partner_rows = arrived.reshape(aux_rows, batch_rows * orb_cols)
    occ_flat = occupied.reshape(aux_rows, batch_rows * orb_cols)
    virt_flat = virtual.reshape(aux_rows, batch_rows * orb_cols)
    self_cols = aux_rows // lax.axis_size("rep")
    own_rows = lax.dynamic_slice_in_dim(virt_flat, rep_index * self_cols, self_cols, 0)
    factor = 1.0 / math.sqrt(batch_rows * orb_cols * lax.axis_size("orb"))
    contract = (((1,), (1,)), ((), ()))
    paired = lax.dot_general(occ_flat, partner_rows, contract, preferred_element_type=jnp.float32)
    diagonal = lax.dot_general(occ_flat, own_rows, contract, preferred_element_type=jnp.float32)
    summed = lax.psum_scatter(
        jnp.concatenate((paired, diagonal), 1) * factor, "orb", scatter_dimension=0, tiled=True
    )
    chi_pair = summed[None, :, :aux_rows]
    chi_self = summed[:, aux_rows:]
    return (chi_pair, chi_self)


def solution(mesh):
    return jax.shard_map(
        per_device,
        mesh=mesh,
        in_specs=(P("aux", None, "orb"), P("orb", None), P("orb", None), P("aux", "orb"), P()),
        out_specs=(P("rep", ("aux", "orb"), None), P(("aux", "orb"), "rep")),
        check_vma=False,
    )
```

profile of v0, /device:TPU:0, one launch (start us, length us, event | category | flops | bytes accessed | tf_op | source)
XLA Modules:
  0.0 172.6 jit_solution(13626867502356585046)
XLA Ops:
  7.2 0.0 copy-start
  7.2 0.7 convert_element_type.9
  7.9 0.6 broadcast_in_dim.20
  8.6 0.1 copy.35
  8.6 2.9 %broadcast_multiply_fusion = bf16[512,4,512]{2,1,0:T(4,128)(2,1)S(1)} fusion(bf16[512,4,512]{2,1,0:T(4,128)(2,1)} %param.5, bf16[512,512]{1,0:T(8,128)(2,1)S(1)} %bitcast.30), kind=kLoop, calls=%fused_computation.9 | loop fusion | flops 1048576 | bytes 4718592 | tf_op jit(solution)/shard_map/mul | solution.py:17
  11.5 0.0 copy-done
  11.5 0.0 copy-start.1
  11.5 1.3 convolution_convert_fusion
  12.8 0.0 copy-done.1
  12.8 1.5 copy.21
  14.3 0.0 copy-start.4
  14.3 6.5 %all-to-all-start = ((bf16[8,64,4,512]{3,1,2,0:T(8,128)(2,1)}), bf16[8,64,4,512]{3,1,2,0:T(8,128)(2,1)}, u32[]{:S(2)}, u32[]{:S(2)}) async-start(bf16[8,64,4,512]{3,1,2,0:T(8,128)(2,1)} %copy.21), calls=%async_computation | async-start | bytes 4194304 | tf_op jit(solution)/shard_map/all_to_all | solution.py:27
  20.8 0.0 copy-done.4
  20.9 49.1 %all-to-all-done = bf16[8,64,4,512]{3,1,2,0:T(8,128)(2,1)} async-done(((bf16[8,64,4,512]{3,1,2,0:T(8,128)(2,1)}), bf16[8,64,4,512]{3,1,2,0:T(8,128)(2,1)}, u32[]{:S(2)}, u32[]{:S(2)}) %all-to-all-start) | async-done | bytes 2097184 | tf_op jit(solution)/shard_map/all_to_all | solution.py:27
  70.0 3.6 %gather_fusion = bf16[8,64,4,512]{3,1,2,0:T(8,128)(2,1)} fusion(bf16[8,64,4,512]{3,1,2,0:T(8,128)(2,1)} %all-to-all-done, s32[1024]{0:T(1024)S(1)} %pad_clamp_fusion), kind=kCustom, calls=%fused_computation | custom fusion | bytes 4194336 | tf_op jit(solution)/shard_map/jit(_take)/gather | solution.py:26
  73.6 3.2 %broadcast_select_fusion = bf16[8,64,4,512]{3,1,2,0:T(8,128)(2,1)} fusion(bf16[8,64,4,512]{3,1,2,0:T(8,128)(2,1)} %gather_fusion, pred[8]{0:T(512)(128)(4,1)S(1)} %compare_and_fusion), kind=kLoop, calls=%fused_computation.1 | loop fusion | flops 1048576 | bytes 4194312 | tf_op jit(solution)/shard_map/jit(_take)/select_n | solution.py:26
  76.8 4.3 %all-to-all-start.1 = ((bf16[8,64,4,512]{3,1,2,0:T(8,128)(2,1)}), bf16[8,64,4,512]{3,1,2,0:T(8,128)(2,1)}, u32[]{:S(2)}, u32[]{:S(2)}) async-start(bf16[8,64,4,512]{3,1,2,0:T(8,128)(2,1)} %broadcast_select_fusion), calls=%async_computation.1 | async-start | bytes 4194304 | tf_op jit(solution)/shard_map/all_to_all | solution.py:29
  81.1 0.0 copy-start.3
  81.1 0.0 reduce-scatter.2.cloned.1.call-start
  81.2 2.4 %copy.23 = bf16[512,4,512]{0,2,1:T(8,128)(2,1)} copy(bf16[512,4,512]{2,0,1:T(8,128)(2,1)S(1)} %convolution_convert_fusion) | data formatting | bytes 4194304 | tf_op jit(solution)/shard_map/convert_element_type | solution.py:23
  83.6 0.0 copy-done.3
  83.6 0.0 copy-start.2
  83.6 3.1 %convolution_convert_fusion.1 = bf16[512,4,512]{0,2,1:T(8,128)(2,1)S(1)} fusion(bf16[512,4,512]{2,1,0:T(4,128)(2,1)} %copy-done.1, bf16[512,512]{1,0:T(8,128)(2,1)S(1)} %copy-done.3), kind=kOutput, calls=%fused_computation.3 | convolution fusion | flops 1074790400 | bytes 4718592 | tf_op jit(solution)/shard_map/plu,ut->plt/dot_general | solution.py:18
  86.7 0.0 copy-start.5
  86.7 1.3 copy-done.5
  88.0 0.0 copy-done.2
  88.0 0.8 fusion.2
  88.8 41.4 %all-to-all-done.1 = bf16[8,64,4,512]{3,1,2,0:T(8,128)(2,1)} async-done(((bf16[8,64,4,512]{3,1,2,0:T(8,128)(2,1)}), bf16[8,64,4,512]{3,1,2,0:T(8,128)(2,1)}, u32[]{:S(2)}, u32[]{:S(2)}) %all-to-all-start.1) | async-done | bytes 2097184 | tf_op jit(solution)/shard_map/all_to_all | solution.py:29
  130.2 3.2 %copy.22 = bf16[8,64,4,512]{3,2,1,0:T(4,128)(2,1)S(1)} copy(bf16[8,64,4,512]{3,1,2,0:T(8,128)(2,1)} %all-to-all-done.1) | data formatting | bytes 4194304 | tf_op jit(solution)/shard_map/all_to_all | solution.py:29
  133.4 0.0 copy-start.6
  133.4 0.6 copy.29
  134.0 1.0 copy-done.6
  135.0 1.2 fusion.8
  136.2 1.4 maximum_multiply_fusion
  137.6 0.0 reduce-scatter.2.cloned.1.call-update
  137.6 25.2 %reduce-scatter.2.cloned.1.call-done = f32[256,768]{0,1:T(8,128)} async-done(((f32[512,768]{0,1:T(8,128)}), f32[256,768]{0,1:T(8,128)}) %reduce-scatter.2.cloned.1.call-update) | async-done | bytes 786448 | tf_op jit(solution)/shard_map/reduce_scatter | solution.py:39
  162.8 0.0 slice-start
  162.8 1.1 slice_bitcast_fusion
  163.9 1.0 copy.24
  164.9 0.0 slice-done
  164.9 0.8 copy.25
  (4 shorter events, 0.1 us)
Async XLA Ops:
  7.2 4.3 %copy-start = (bf16[512,512]{1,0:T(8,128)(2,1)S(1)}, bf16[512,512]{1,0:T(8,128)(2,1)}, u32[]{:S(2)}) copy-start(bf16[512,512]{1,0:T(8,128)(2,1)} %param.7) | copy-start | bytes 1572868
  11.5 1.3 copy-start.1
  14.3 6.5 %copy-start.4 = (s32[2,8]{1,0:T(2,128)S(1)}, s32[2,8]{1,0:T(2,128)}, u32[]{:S(2)}) copy-start(s32[2,8]{1,0:T(2,128)} %param.9) | copy-start | bytes 196
  14.3 55.6 %all-to-all-start = ((bf16[8,64,4,512]{3,1,2,0:T(8,128)(2,1)}), bf16[8,64,4,512]{3,1,2,0:T(8,128)(2,1)}, u32[]{:S(2)}, u32[]{:S(2)}) async-start(bf16[8,64,4,512]{3,1,2,0:T(8,128)(2,1)} %copy.21), calls=%async_computation | async-start | bytes 4194304 | tf_op jit(solution)/shard_map/all_to_all | solution.py:27
  76.8 53.4 %all-to-all-start.1 = ((bf16[8,64,4,512]{3,1,2,0:T(8,128)(2,1)}), bf16[8,64,4,512]{3,1,2,0:T(8,128)(2,1)}, u32[]{:S(2)}, u32[]{:S(2)}) async-start(bf16[8,64,4,512]{3,1,2,0:T(8,128)(2,1)} %broadcast_select_fusion), calls=%async_computation.1 | async-start | bytes 4194304 | tf_op jit(solution)/shard_map/all_to_all | solution.py:29
  81.1 2.4 %copy-start.3 = (bf16[512,512]{1,0:T(8,128)(2,1)S(1)}, bf16[512,512]{1,0:T(8,128)(2,1)}, u32[]{:S(2)}) copy-start(bf16[512,512]{1,0:T(8,128)(2,1)} %param.6) | copy-start | bytes 1572868
  81.1 81.7 %reduce-scatter.2.cloned.1.call-start = ((), (), s32[]{:S(2)}) async-start(), calls=%async_computation.3 | async-start | bytes 2359296 | tf_op jit(solution)/shard_map/reduce_scatter | solution.py:39
  83.6 4.5 %copy-start.2 = (bf16[512,4,512]{0,2,1:T(8,128)(2,1)S(1)}, bf16[512,4,512]{0,2,1:T(8,128)(2,1)}, u32[]{:S(2)}) copy-start(bf16[512,4,512]{0,2,1:T(8,128)(2,1)} %copy.23) | copy-start | bytes 6291460
  86.7 1.3 copy-start.5
  133.4 1.6 copy-start.6
  162.8 2.1 %slice-start = ((f32[256,768]{0,1:T(8,128)}), f32[256,256]{0,1:T(8,128)S(1)}, s32[]{:S(2)}) async-start(f32[256,768]{0,1:T(8,128)} %reduce-scatter.2.cloned.1.call-done), calls=%async_computation.4 | async-start | bytes 524288 | tf_op jit(solution)/shard_map/slice | solution.py:43
Sparse Core Ops, SparseCore 0:
  137.7 25.0 reduce-scatter.1
where the time goes:
time: 173 us
  waiting for transfers between devices  116 us (67%)
  local copies, waits for them, and re-layouts  17.3 us (10%)
  between operations  14.2 us (8%)
  starting transfers between devices  10.9 us (6%)
  other arithmetic  8.2 us (5%)
  matrix products  6.39 us (4%)
    all_to_all x1, waiting for transfers between devices, per_device(): lax.all_to_all(pieces, 'aux', split_axis=0, concat_axis=0, tiled=True)  49.1 us
    all_to_all x1, waiting for transfers between devices, per_device(): lax.all_to_all(reordered, 'aux', split_axis=0, concat_axis=0, tiled=True)  41.4 us
    reduce_scatter x1, waiting for transfers between devices, per_device(): lax.psum_scatter(jnp.concatenate((paired, diagonal), 1) * factor, 'orb',...  25.2 us
    all_to_all x1, starting transfers between devices, per_device(): lax.all_to_all(pieces, 'aux', split_axis=0, concat_axis=0, tiled=True)  6.49 us
    unnamed x18, local copies, waits for them, and re-layouts  4.88 us
    all_to_all x1, starting transfers between devices, per_device(): lax.all_to_all(reordered, 'aux', split_axis=0, concat_axis=0, tiled=True)  4.34 us
    gather x1, local copies, waits for them, and re-layouts, per_device(): jnp.take(lax.all_to_all(pieces, 'aux', split_axis=0, concat_axis=0, tiled...  3.61 us
  transfers between devices with their start and end apart: 3, of which 3 were waited for; matrix products, arithmetic and copies ran while one was open for 4% of the time, Pallas kernels for 0%

commit v1 on v0

v1 whole, which is shorter than its diff:
```python
import functools
import math

import jax
import jax.numpy as jnp
from jax import lax
from jax.experimental import pallas as pl
from jax.experimental.pallas import tpu as pltpu
from jax.sharding import PartitionSpec as P

BLOCK = 128
MESH = pl.DeviceIdType.MESH
CONTRACT = (((1,), (1,)), ((), ()))


def kernel(sizes, factor, match_ref, masked, occ_dens, virt_dens, pair_out, self_out, *scratch):
    chips, orbs, reps, pieces, groups, rows_piece, half = sizes
    gath = scratch[:pieces]
    (occ, chosen, other, ends, tiles, arrived, self_tile, self_arrived,
     recv_sem, up_sem, down_sem, core_send, core_recv, local_sem, end_send, end_recv,
     rep_send, rep_recv, orb_send, orb_recv) = scratch[pieces:]
    per_group = pieces // groups
    cols_group = per_group * rows_piece
    batch, aux_rows, orb_cols = masked.shape
    rows_out = aux_rows // orbs
    self_cols = aux_rows // reps

    a = lax.axis_index("aux")
    o = lax.axis_index("orb")
    r = lax.axis_index("rep")
    z = a // 2
    k = a % 2
    far = (r + 1) % reps
    inner = jnp.logical_and(z >= 1, z <= chips - 2)
    at_end = jnp.logical_or(z == 0, z == chips - 1)
    up_ok = z + 1 <= chips - 2
    down_ok = z - 1 >= 1
    feeds = jnp.logical_or(z == 1, z == chips - 2)
    end_aux = jnp.where(z == 1, k, 2 * (chips - 1) + k)

    barrier = pltpu.get_barrier_semaphore()

    @pl.when(z > 0)
    def _():
        pl.semaphore_signal(barrier, inc=1, device_id={"aux": a - 2}, device_id_type=MESH)

    @pl.when(z < chips - 1)
    def _():
        pl.semaphore_signal(barrier, inc=1, device_id={"aux": a + 2}, device_id_type=MESH)

    pl.semaphore_signal(barrier, inc=1, device_id={"aux": 2 * z + 1 - k}, device_id_type=MESH)
    pl.semaphore_signal(barrier, inc=1, device_id={"rep": far}, device_id_type=MESH)
    for j in range(1, orbs):
        pl.semaphore_signal(barrier, inc=1, device_id={"orb": (o + j) % orbs}, device_id_type=MESH)
    pl.semaphore_wait(barrier, 2 + orbs - 1 + jnp.where(at_end, 1, 2))

    def piece(c):
        return masked.at[pl.ds(r * half, half), pl.ds(c * rows_piece, rows_piece), :]

    def remote(src, dst, send, recv, where):
        return pltpu.make_async_remote_copy(
            src_ref=src, dst_ref=dst, send_sem=send, recv_sem=recv, device_id=where, device_id_type=MESH
        )

    def slot(c, zz):
        return gath[c].at[2 * zz + k]

    def up(c, zz, src):
        return remote(src, slot(c, zz), up_sem.at[c, zz], recv_sem.at[c, zz], {"aux": a + 2})

    def down(c, zz, src):
        return remote(src, slot(c, zz), down_sem.at[c, zz], recv_sem.at[c, zz], {"aux": a - 2})

    def cross(c, zz, src):
        return remote(src, slot(c, zz), core_send.at[c, zz], core_recv.at[c, zz], {"aux": 2 * z + 1 - k})

    def local(c):
        return pltpu.make_async_copy(piece(c), gath[c].at[a], local_sem.at[c])

    def span(c):
        return c // per_group, pl.ds((c % per_group) * rows_piece, rows_piece)

    def feed(c):
        g, rows = span(c)
        return remote(ends.at[c], chosen.at[g, :, :, rows, :], end_send.at[c], end_recv.at[c], {"aux": end_aux})

    def swap(c):
        g, rows = span(c)
        return remote(chosen.at[g, 1, :, rows, :], other.at[g, :, rows, :], rep_send.at[c], rep_recv.at[c], {"rep": far})

    def lower(c, send):
        for d in range(1, chips):
            @pl.when(z - d >= 0)
            def _():
                zz = jnp.maximum(z - d, 0)
                up(c, zz, slot(c, zz)).wait_recv()
                if send:
                    up(c, zz, slot(c, zz)).start()
                cross(c, zz, slot(c, zz)).start()

    def upper(c, send):
        for d in range(1, chips):
            @pl.when(z + d <= chips - 1)
            def _():
                zz = jnp.minimum(z + d, chips - 1)
                down(c, zz, slot(c, zz)).wait_recv()
                if send:
                    down(c, zz, slot(c, zz)).start()
                cross(c, zz, slot(c, zz)).start()

    def own(c):
        @pl.when(up_ok)
        def _():
            up(c, z, piece(c)).start()

        @pl.when(down_ok)
        def _():
            down(c, z, piece(c)).start()

        @pl.when(inner)
        def _():
            cross(c, z, piece(c)).start()
            local(c).start()

    def relay(c):
        @pl.when(jnp.logical_and(inner, up_ok))
        def _():
            lower(c, True)

        @pl.when(jnp.logical_and(inner, down_ok))
        def _():
            upper(c, True)

    def complete(c):
        g, rows = span(c)

        @pl.when(inner)
        def _():
            @pl.when(jnp.logical_not(up_ok))
            def _():
                lower(c, False)

            @pl.when(jnp.logical_not(down_ok))
            def _():
                upper(c, False)

            for zz in range(chips):
                remote(gath[c].at[2 * zz + k], gath[c].at[2 * zz + 1 - k], core_send.at[c, zz],
                       core_recv.at[c, zz], {"aux": 2 * z + 1 - k}).wait_recv()
            local(c).wait()

            @pl.when(feeds)
            def _():
                ends[c, 0] = gath[c][match_ref[r, end_aux]]
                ends[c, 1] = gath[c][match_ref[far, end_aux]]

            chosen[g, 1, :, rows, :] = gath[c][match_ref[far, a]]
            chosen[g, 0, :, rows, :] = gath[c][match_ref[r, a]]

            @pl.when(feeds)
            def _():
                feed(c).start()

        @pl.when(at_end)
        def _():
            feed(c).wait_recv()

        swap(c).start()

    def orb_copy(g, j):
        peer = (o + j) % orbs
        return remote(tiles.at[g, pl.ds(peer * rows_out, rows_out), :], arrived.at[g, j - 1],
                      orb_send.at[g, j - 1], orb_recv.at[g, j - 1], {"orb": peer})

    def self_copy(j):
        peer = (o + j) % orbs
        return remote(self_tile.at[pl.ds(peer * rows_out, rows_out), :], self_arrived.at[j - 1],
                      orb_send.at[groups, j - 1], orb_recv.at[groups, j - 1], {"orb": peer})

    def product(l, rows_l):
        moved = jnp.dot(rows_l, virt_dens[...], preferred_element_type=jnp.float32).astype(jnp.bfloat16)
        return lax.dot_general(occ[l], moved, CONTRACT, preferred_element_type=jnp.float32)

    def group(g):
        for c in range(g * per_group, (g + 1) * per_group):
            swap(c).wait_recv()
        total = None
        for i in range(half):
            term = product(r * half + i, chosen[g, 0, i])
            total = term if total is None else total + term
            total = total + product(far * half + i, other[g, i])
        tiles[g] = total * factor
        for j in range(1, orbs):
            orb_copy(g, j).start()

    def finish(g):
        total = tiles[g, pl.ds(o * rows_out, rows_out), :]
        for j in range(1, orbs):
            orb_copy(g, j).wait_recv()
            total = total + arrived[g, j - 1]
        pair_out[:, g * cols_group:(g + 1) * cols_group] = total

    own(0)
    own(1)

    def one_occ(l, carry):
        occ[l] = jnp.dot(masked[l], occ_dens[...], preferred_element_type=jnp.float32).astype(jnp.bfloat16)
        return carry

    relay(0)
    lax.fori_loop(0, batch, one_occ, 0)
    for c in range(pieces):
        if c + 2 < pieces:
            own(c + 2)
        if c + 1 < pieces:
            relay(c + 1)
        complete(c)
        if c == 0:
            total = None
            for l in range(batch):
                term = product(l, masked[l, pl.ds(r * self_cols, self_cols), :])
                total = term if total is None else total + term
            self_tile[...] = total * factor
        if c == 1:
            for j in range(1, orbs):
                self_copy(j).start()
        lag = c - 2
        if lag >= 0 and lag % per_group == per_group - 1:
            g = lag // per_group
            group(g)
            if g > 0:
                finish(g - 1)
    done = (pieces - 2) // per_group if pieces > 2 else 0
    for g in range(done, groups):
        group(g)
        if g > 0:
            finish(g - 1)
    total = self_tile[pl.ds(o * rows_out, rows_out), :]
    for j in range(1, orbs):
        self_copy(j).wait_recv()
        total = total + self_arrived[j - 1]
    self_out[...] = total
    finish(groups - 1)

    for c in range(pieces):
        for d in range(chips):
            @pl.when(jnp.logical_and(up_ok, z - d >= 0))
            def _():
                up(c, jnp.maximum(z - d, 0), piece(c)).wait_send()

            @pl.when(jnp.logical_and(down_ok, z + d <= chips - 1))
            def _():
                down(c, jnp.minimum(z + d, chips - 1), piece(c)).wait_send()

        @pl.when(inner)
        def _():
            for zz in range(chips):
                cross(c, zz, piece(c)).wait_send()

        @pl.when(feeds)
        def _():
            feed(c).wait_send()

        swap(c).wait_send()
    for j in range(1, orbs):
        self_copy(j).wait_send()
        for g in range(groups):
            orb_copy(g, j).wait_send()


def per_device(slab, occ_density, virt_density, block_mask, matching):
    owners = lax.axis_size("aux")
    orbs = lax.axis_size("orb")
    reps = lax.axis_size("rep")
    chips = owners // 2
    aux_rows, batch, orb_cols = slab.shape
    pieces = max(2, 32 // chips)
    rows_piece = aux_rows // pieces
    per_group = max(1, BLOCK // rows_piece)
    groups = pieces // per_group
    cols_group = per_group * rows_piece
    half = batch // reps
    rows_out = aux_rows // orbs
    self_cols = aux_rows // reps
    weights = block_mask.astype(jnp.bfloat16)
    spread = jnp.repeat(jnp.repeat(weights, BLOCK, axis=0), BLOCK, axis=1)
    masked = jnp.transpose(slab, (1, 0, 2)) * spread[None]
    factor = 1.0 / math.sqrt(batch * orb_cols * orbs)
    dma = pltpu.SemaphoreType.DMA
    vmem = pl.BlockSpec(memory_space=pltpu.VMEM)
    bf16, f32 = jnp.bfloat16, jnp.float32
    pair, own = pl.pallas_call(
        functools.partial(kernel, (chips, orbs, reps, pieces, groups, rows_piece, half), factor),
        out_shape=(
            jax.ShapeDtypeStruct((rows_out, aux_rows), f32),
            jax.ShapeDtypeStruct((rows_out, self_cols), f32),
        ),
        in_specs=[pl.BlockSpec(memory_space=pltpu.SMEM), vmem, vmem, vmem],
        out_specs=(vmem, vmem),
        scratch_shapes=[pltpu.VMEM((owners, half, rows_piece, orb_cols), bf16) for _ in range(pieces)] + [
            pltpu.VMEM((batch, aux_rows, orb_cols), bf16),
            pltpu.VMEM((groups, 2, half, cols_group, orb_cols), bf16),
            pltpu.VMEM((groups, half, cols_group, orb_cols), bf16),
            pltpu.VMEM((pieces, 2, half, rows_piece, orb_cols), bf16),
            pltpu.VMEM((groups, aux_rows, cols_group), f32),
            pltpu.VMEM((groups, orbs - 1, rows_out, cols_group), f32),
            pltpu.VMEM((aux_rows, self_cols), f32),
            pltpu.VMEM((orbs - 1, rows_out, self_cols), f32),
            dma((pieces, chips)), dma((pieces, chips)), dma((pieces, chips)),
            dma((pieces, chips)), dma((pieces, chips)),
            dma((pieces,)), dma((pieces,)), dma((pieces,)), dma((pieces,)), dma((pieces,)),
            dma((groups + 1, orbs - 1)), dma((groups + 1, orbs - 1)),
        ],
        compiler_params=pltpu.CompilerParams(
            collective_id=0, has_side_effects=True, vmem_limit_bytes=56 * 2**20
        ),
    )(matching, masked, occ_density, virt_density)
    return (pair[None], own)


def solution(mesh):
    return jax.shard_map(
        per_device,
        mesh=mesh,
        in_specs=(P("aux", None, "orb"), P("orb", None), P("orb", None), P("aux", "orb"), P()),
        out_specs=(P("rep", ("aux", "orb"), None), P(("aux", "orb"), "rep")),
        check_vma=False,
    )
```

time: 173 us -> 95.5 us (0.55)
  waiting for transfers between devices: 116 us -> 0 us
  Pallas kernels: 0 us -> 86 us
  between operations: 14.2 us -> 0.66 us
  local copies, waits for them, and re-layouts: 17.3 us -> 4.24 us
  starting transfers between devices: 10.9 us -> 0 us
  matrix products: 6.39 us -> 0 us
  other arithmetic: 8.2 us -> 4.36 us
    all_to_all x2 -> x0, waiting for transfers between devices: 90.5 us -> none  [the longest x1 49.1 us: per_device(): lax.all_to_all(pieces, 'aux', split_axis=0, concat_axis=0, tiled=True)]
    pallas_call x0 -> x1, Pallas kernels: none -> 86 us  [per_device(): pl.pallas_call(functools.partial(kernel, (chips, orbs, reps, pieces, grou...]
    reduce_scatter x1 -> x0, waiting for transfers between devices: 25.2 us -> none  [per_device(): lax.psum_scatter(jnp.concatenate((paired, diagonal), 1) * factor, 'orb',...]
    all_to_all x2 -> x0, starting transfers between devices: 10.8 us -> none  [the longest x1 6.49 us: per_device(): lax.all_to_all(pieces, 'aux', split_axis=0, concat_axis=0, tiled=True)]
    dot_general x4 -> x0, matrix products: 6.39 us -> none  [the longest x1 3.13 us: per_device(): jnp.einsum('plu,ut->plt', masked, occ_density, preferred_element_type=jnp...]
    gather x1 -> x0, local copies, waits for them, and re-layouts: 3.61 us -> none  [per_device(): jnp.take(lax.all_to_all(pieces, 'aux', split_axis=0, concat_axis=0, tiled...]
    all_to_all x1 -> x0, local copies, waits for them, and re-layouts: 3.22 us -> none  [per_device(): lax.all_to_all(reordered, 'aux', split_axis=0, concat_axis=0, tiled=True)]
    select_n x2 -> x0, other arithmetic: 3.21 us -> none  [per_device(): jnp.take(lax.all_to_all(pieces, 'aux', split_axis=0, concat_axis=0, tiled...]
  transfers between devices with their start and end apart: 3 -> 0, of which waited for: 3 -> 0; matrix products, arithmetic and copies ran while one was open for 4% -> 0% of each run, Pallas kernels for 0% -> 0%
where the time goes in v1:
time: 95.5 us; the launch traced here: 95.3 us
  Pallas kernels  86 us (90%)
  other arithmetic  4.36 us (5%)
  local copies, waits for them, and re-layouts  4.24 us (4%)
    pallas_call x1, Pallas kernels, per_device(): pl.pallas_call(functools.partial(kernel, (chips, orbs, reps, pieces, grou...  86 us
    mul x1, other arithmetic, per_device(): masked = jnp.transpose(slab, (1, 0, 2)) * spread[None]  3.67 us
    unnamed x3, local copies, waits for them, and re-layouts  3.62 us

profile of v1, /device:TPU:0, one launch (start us, length us, event | category | flops | bytes accessed | tf_op | source)
XLA Modules:
  0.0 95.3 jit_solution(1537102961725843683)
XLA Ops:
  0.6 0.7 convert_element_type.3
  1.3 0.6 broadcast_in_dim.10
  1.9 0.1 copy.13
  2.0 3.7 %fusion.masked = bf16[4,512,512]{2,1,0:T(8,128)(2,1)} fusion(bf16[512,4,512]{2,1,0:T(4,128)(2,1)} %param.5, bf16[512,512]{1,0:T(8,128)(2,1)S(1)} %bitcast.8), kind=kLoop, calls=%fused_computation.1 | loop fusion | flops 1048576 | bytes 4718592 | tf_op jit(solution)/shard_map/mul | solution.py:287
  5.7 86.0 %shard_map.68 = (f32[256,512]{1,0:T(8,128)}, f32[256,256]{1,0:T(8,128)}) custom-call(s32[2,8]{1,0:T(2,128)} %match_ref.1, bf16[4,512,512]{2,1,0:T(8,128)(2,1)} %fusion.masked, bf16[512,512]{1,0:T(8,128)(2,1)} %occ_dens.1, bf16[512,512]{1,0:T(8,128)(2,1)} %virt_dens.1), custom_call_target="tpu_custom_call" | custom-call | tf_op jit(solution)/shard_map/pallas_call | solution.py:292
  91.7 1.9 %copy.16 = f32[1,256,512]{2,1,0:T(8,128)} copy(f32[1,256,512]{2,1,0:T(8,128)} %bitcast.11) | data formatting | bytes 1048576
  93.6 1.7 %copy.17 = f32[256,256]{1,0:T(8,128)} copy(f32[256,256]{1,0:T(8,128)} %get-tuple-element.9) | data formatting | bytes 524288
  (1 shorter events, 0.0 us)

commit v2 on v1

--- a/solution.py
+++ b/solution.py
@@ -16,9 +16,9 @@
 def kernel(sizes, factor, match_ref, masked, occ_dens, virt_dens, pair_out, self_out, *scratch):
     chips, orbs, reps, pieces, groups, rows_piece, half = sizes
     gath = scratch[:pieces]
-    (occ, chosen, other, ends, tiles, arrived, self_tile, self_arrived,
+    (occ, parts, whole, arrived, ends, landed, self_tile, self_arrived,
      recv_sem, up_sem, down_sem, core_send, core_recv, local_sem, end_send, end_recv,
-     rep_send, rep_recv, orb_send, orb_recv) = scratch[pieces:]
+     part_send, part_recv, self_send, self_recv) = scratch[pieces:]
     per_group = pieces // groups
     cols_group = per_group * rows_piece
     batch, aux_rows, orb_cols = masked.shape
@@ -30,7 +30,11 @@
     r = lax.axis_index("rep")
     z = a // 2
     k = a % 2
-    far = (r + 1) % reps
+
+    def peer(j):
+        to_orb, to_rep = (o + j // reps) % orbs, (r + j % reps) % reps
+        return to_orb, to_rep, {"orb": to_orb, "rep": to_rep}
+
     inner = jnp.logical_and(z >= 1, z <= chips - 2)
     at_end = jnp.logical_or(z == 0, z == chips - 1)
     up_ok = z + 1 <= chips - 2
@@ -49,10 +53,9 @@
         pl.semaphore_signal(barrier, inc=1, device_id={"aux": a + 2}, device_id_type=MESH)
 
     pl.semaphore_signal(barrier, inc=1, device_id={"aux": 2 * z + 1 - k}, device_id_type=MESH)
-    pl.semaphore_signal(barrier, inc=1, device_id={"rep": far}, device_id_type=MESH)
-    for j in range(1, orbs):
-        pl.semaphore_signal(barrier, inc=1, device_id={"orb": (o + j) % orbs}, device_id_type=MESH)
-    pl.semaphore_wait(barrier, 2 + orbs - 1 + jnp.where(at_end, 1, 2))
+    for j in range(1, orbs * reps):
+        pl.semaphore_signal(barrier, inc=1, device_id=peer(j)[2], device_id_type=MESH)
+    pl.semaphore_wait(barrier, orbs * reps + jnp.where(at_end, 1, 2))
 
     def piece(c):
         return masked.at[pl.ds(r * half, half), pl.ds(c * rows_piece, rows_piece), :]
@@ -76,17 +79,6 @@
 
     def local(c):
         return pltpu.make_async_copy(piece(c), gath[c].at[a], local_sem.at[c])
-
-    def span(c):
-        return c // per_group, pl.ds((c % per_group) * rows_piece, rows_piece)
-
-    def feed(c):
-        g, rows = span(c)
-        return remote(ends.at[c], chosen.at[g, :, :, rows, :], end_send.at[c], end_recv.at[c], {"aux": end_aux})
-
-    def swap(c):
-        g, rows = span(c)
-        return remote(chosen.at[g, 1, :, rows, :], other.at[g, :, rows, :], rep_send.at[c], rep_recv.at[c], {"rep": far})
 
     def lower(c, send):
         for d in range(1, chips):
@@ -132,8 +124,6 @@
             upper(c, True)
 
     def complete(c):
-        g, rows = span(c)
-
         @pl.when(inner)
         def _():
             @pl.when(jnp.logical_not(up_ok))
@@ -144,76 +134,106 @@
             def _():
                 upper(c, False)
 
-            for zz in range(chips):
-                remote(gath[c].at[2 * zz + k], gath[c].at[2 * zz + 1 - k], core_send.at[c, zz],
-                       core_recv.at[c, zz], {"aux": 2 * z + 1 - k}).wait_recv()
-            local(c).wait()
-
-            @pl.when(feeds)
-            def _():
-                ends[c, 0] = gath[c][match_ref[r, end_aux]]
-                ends[c, 1] = gath[c][match_ref[far, end_aux]]
-
-            chosen[g, 1, :, rows, :] = gath[c][match_ref[far, a]]
-            chosen[g, 0, :, rows, :] = gath[c][match_ref[r, a]]
-
-            @pl.when(feeds)
-            def _():
-                feed(c).start()
-
-        @pl.when(at_end)
-        def _():
-            feed(c).wait_recv()
-
-        swap(c).start()
-
-    def orb_copy(g, j):
-        peer = (o + j) % orbs
-        return remote(tiles.at[g, pl.ds(peer * rows_out, rows_out), :], arrived.at[g, j - 1],
-                      orb_send.at[g, j - 1], orb_recv.at[g, j - 1], {"orb": peer})
+    def part_copy(g, t, j):
+        to_orb, to_rep, where = peer(j)
+        return remote(parts.at[g, t, to_rep, pl.ds(to_orb * rows_out, rows_out), :], arrived.at[g, t, j - 1],
+                      part_send.at[g, t, j - 1], part_recv.at[g, t, j - 1], where)
+
+    def feed(g):
+        return remote(ends.at[g], landed.at[g], end_send.at[g], end_recv.at[g], {"aux": end_aux})
 
     def self_copy(j):
-        peer = (o + j) % orbs
-        return remote(self_tile.at[pl.ds(peer * rows_out, rows_out), :], self_arrived.at[j - 1],
-                      orb_send.at[groups, j - 1], orb_recv.at[groups, j - 1], {"orb": peer})
+        to_orb = (o + j) % orbs
+        return remote(self_tile.at[pl.ds(to_orb * rows_out, rows_out), :], self_arrived.at[j - 1],
+                      self_send.at[j - 1], self_recv.at[j - 1], {"orb": to_orb})
 
     def product(l, rows_l):
         moved = jnp.dot(rows_l, virt_dens[...], preferred_element_type=jnp.float32).astype(jnp.bfloat16)
         return lax.dot_general(occ[l], moved, CONTRACT, preferred_element_type=jnp.float32)
 
+    def end_occ(c):
+        @pl.when(feeds)
+        def _():
+            rows_e = gath[c][end_aux].reshape(half * rows_piece, orb_cols)
+            made = jnp.dot(rows_e, occ_dens[...], preferred_element_type=jnp.float32).astype(jnp.bfloat16)
+            occ[batch:, c * rows_piece:(c + 1) * rows_piece, :] = made.reshape(half, rows_piece, orb_cols)
+
     def group(g):
-        for c in range(g * per_group, (g + 1) * per_group):
-            swap(c).wait_recv()
-        total = None
-        for i in range(half):
-            term = product(r * half + i, chosen[g, 0, i])
-            total = term if total is None else total + term
-            total = total + product(far * half + i, other[g, i])
-        tiles[g] = total * factor
-        for j in range(1, orbs):
-            orb_copy(g, j).start()
+        span = range(g * per_group, (g + 1) * per_group)
+
+        @pl.when(inner)
+        def _():
+            for c in span:
+                for zz in range(chips):
+                    remote(gath[c].at[2 * zz + k], gath[c].at[2 * zz + 1 - k], core_send.at[c, zz],
+                           core_recv.at[c, zz], {"aux": 2 * z + 1 - k}).wait_recv()
+                local(c).wait()
+
+            def one_tile(n, carry):
+                t, turn = n // reps, n % reps
+                owner = jnp.where(t == 0, a, end_aux)
+                first = jnp.where(t == 0, r * half, batch)
+                partner = match_ref[turn, owner]
+                total = None
+                for i in range(half):
+                    rows_l = [gath[c][partner, i] for c in span]
+                    rows_l = rows_l[0] if per_group == 1 else jnp.concatenate(rows_l, 0)
+                    term = product(first + i, rows_l)
+                    total = term if total is None else total + term
+                total = total * factor
+                parts[g, t, turn] = total.astype(jnp.bfloat16)
+                whole[g, t, turn] = total
+                return carry
+
+            lax.fori_loop(0, jnp.where(feeds, 2 * reps, reps), one_tile, 0)
+            for j in range(1, orbs * reps):
+                @pl.when(feeds)
+                def _():
+                    part_copy(g, 1, j).start()
+            for j in range(1, orbs * reps):
+                part_copy(g, 0, j).start()
+
+    def summed(g, t):
+        total = whole[g, t, r, pl.ds(o * rows_out, rows_out), :]
+        for j in range(1, orbs * reps):
+            part_copy(g, t, j).wait_recv()
+            total = total + arrived[g, t, j - 1].astype(jnp.float32)
+        return total
 
     def finish(g):
-        total = tiles[g, pl.ds(o * rows_out, rows_out), :]
-        for j in range(1, orbs):
-            orb_copy(g, j).wait_recv()
-            total = total + arrived[g, j - 1]
-        pair_out[:, g * cols_group:(g + 1) * cols_group] = total
-
-    own(0)
-    own(1)
+        @pl.when(inner)
+        def _():
+            @pl.when(feeds)
+            def _():
+                ends[g] = summed(g, 1)
+                feed(g).start()
+
+            pair_out[:, g * cols_group:(g + 1) * cols_group] = summed(g, 0)
+
+    ahead = 2
+    ready = 0
+    closed = 0
 
     def one_occ(l, carry):
         occ[l] = jnp.dot(masked[l], occ_dens[...], preferred_element_type=jnp.float32).astype(jnp.bfloat16)
         return carry
 
-    relay(0)
+    own(0)
+    own(1)
     lax.fori_loop(0, batch, one_occ, 0)
+    for c in range(min(ahead, pieces)):
+        relay(c)
+        end_occ(c)
     for c in range(pieces):
         if c + 2 < pieces:
             own(c + 2)
-        if c + 1 < pieces:
-            relay(c + 1)
+        if c + ahead < pieces:
+            relay(c + ahead)
+            end_occ(c + ahead)
+        filled = c + ahead >= pieces - 1
+        if filled and (ready + 1) * per_group <= c:
+            group(ready)
+            ready += 1
         complete(c)
         if c == 0:
             total = None
@@ -224,23 +244,27 @@
         if c == 1:
             for j in range(1, orbs):
                 self_copy(j).start()
-        lag = c - 2
-        if lag >= 0 and lag % per_group == per_group - 1:
-            g = lag // per_group
-            group(g)
-            if g > 0:
-                finish(g - 1)
-    done = (pieces - 2) // per_group if pieces > 2 else 0
-    for g in range(done, groups):
+        if filled and c == pieces - 2 and closed + 1 < ready:
+            finish(closed)
+            closed += 1
+        if filled and c < pieces - 1 and (ready + 1) * per_group <= c + 1:
+            group(ready)
+            ready += 1
+    for g in range(ready, groups):
         group(g)
-        if g > 0:
-            finish(g - 1)
     total = self_tile[pl.ds(o * rows_out, rows_out), :]
     for j in range(1, orbs):
         self_copy(j).wait_recv()
         total = total + self_arrived[j - 1]
     self_out[...] = total
-    finish(groups - 1)
+    for g in range(closed, groups):
+        finish(g)
+
+    @pl.when(at_end)
+    def _():
+        for g in range(groups):
+            feed(g).wait_recv()
+            pair_out[:, g * cols_group:(g + 1) * cols_group] = landed[g]
 
     for c in range(pieces):
         for d in range(chips):
@@ -257,15 +281,19 @@
             for zz in range(chips):
                 cross(c, zz, piece(c)).wait_send()
 
-        @pl.when(feeds)
-        def _():
-            feed(c).wait_send()
-
-        swap(c).wait_send()
     for j in range(1, orbs):
         self_copy(j).wait_send()
-        for g in range(groups):
-            orb_copy(g, j).wait_send()
+    for g in range(groups):
+        @pl.when(inner)
+        def _():
+            for j in range(1, orbs * reps):
+                part_copy(g, 0, j).wait_send()
+
+        @pl.when(feeds)
+        def _():
+            for j in range(1, orbs * reps):
+                part_copy(g, 1, j).wait_send()
+            feed(g).wait_send()
 
 
 def per_device(slab, occ_density, virt_density, block_mask, matching):
@@ -298,18 +326,19 @@
         in_specs=[pl.BlockSpec(memory_space=pltpu.SMEM), vmem, vmem, vmem],
         out_specs=(vmem, vmem),
         scratch_shapes=[pltpu.VMEM((owners, half, rows_piece, orb_cols), bf16) for _ in range(pieces)] + [
-            pltpu.VMEM((batch, aux_rows, orb_cols), bf16),
-            pltpu.VMEM((groups, 2, half, cols_group, orb_cols), bf16),
-            pltpu.VMEM((groups, half, cols_group, orb_cols), bf16),
-            pltpu.VMEM((pieces, 2, half, rows_piece, orb_cols), bf16),
-            pltpu.VMEM((groups, aux_rows, cols_group), f32),
-            pltpu.VMEM((groups, orbs - 1, rows_out, cols_group), f32),
+            pltpu.VMEM((batch + half, aux_rows, orb_cols), bf16),
+            pltpu.VMEM((groups, 2, reps, aux_rows, cols_group), bf16),
+            pltpu.VMEM((groups, 2, reps, aux_rows, cols_group), f32),
+            pltpu.VMEM((groups, 2, orbs * reps - 1, rows_out, cols_group), bf16),
+            pltpu.VMEM((groups, rows_out, cols_group), f32),
+            pltpu.VMEM((groups, rows_out, cols_group), f32),
             pltpu.VMEM((aux_rows, self_cols), f32),
             pltpu.VMEM((orbs - 1, rows_out, self_cols), f32),
             dma((pieces, chips)), dma((pieces, chips)), dma((pieces, chips)),
             dma((pieces, chips)), dma((pieces, chips)),
-            dma((pieces,)), dma((pieces,)), dma((pieces,)), dma((pieces,)), dma((pieces,)),
-            dma((groups + 1, orbs - 1)), dma((groups + 1, orbs - 1)),
+            dma((pieces,)), dma((groups,)), dma((groups,)),
+            dma((groups, 2, orbs * reps - 1)), dma((groups, 2, orbs * reps - 1)),
+            dma((orbs - 1,)), dma((orbs - 1,)),
         ],
         compiler_params=pltpu.CompilerParams(
             collective_id=0, has_side_effects=True, vmem_limit_bytes=56 * 2**20

time: 95.5 us -> 79.5 us (0.83)
  Pallas kernels: 86 us -> 69.9 us
    pallas_call x1, Pallas kernels: 86 us -> 69.9 us  [per_device(): pl.pallas_call(functools.partial(kernel, (chips, orbs, reps, pieces, grou...]
where the time goes in v2:
time: 79.5 us; the launch traced here: 79.2 us
  Pallas kernels  69.9 us (88%)
  other arithmetic  4.36 us (5%)
  local copies, waits for them, and re-layouts  4.24 us (5%)
    pallas_call x1, Pallas kernels, per_device(): pl.pallas_call(functools.partial(kernel, (chips, orbs, reps, pieces, grou...  69.9 us
    mul x1, other arithmetic, per_device(): masked = jnp.transpose(slab, (1, 0, 2)) * spread[None]  3.67 us
    unnamed x3, local copies, waits for them, and re-layouts  3.62 us

profile of v2, /device:TPU:0, one launch (start us, length us, event | category | flops | bytes accessed | tf_op | source)
XLA Modules:
  0.0 79.2 jit_solution(11930154082353477521)
XLA Ops:
  0.6 0.7 convert_element_type.3
  1.3 0.6 broadcast_in_dim.10
  1.9 0.1 copy.13
  2.0 3.7 %fusion.masked = bf16[4,512,512]{2,1,0:T(8,128)(2,1)} fusion(bf16[512,4,512]{2,1,0:T(4,128)(2,1)} %param.5, bf16[512,512]{1,0:T(8,128)(2,1)S(1)} %bitcast.8), kind=kLoop, calls=%fused_computation.1 | loop fusion | flops 1048576 | bytes 4718592 | tf_op jit(solution)/shard_map/mul | solution.py:315
  5.7 69.9 %shard_map.68 = (f32[256,512]{1,0:T(8,128)}, f32[256,256]{1,0:T(8,128)}) custom-call(s32[2,8]{1,0:T(2,128)} %match_ref.1, bf16[4,512,512]{2,1,0:T(8,128)(2,1)} %fusion.masked, bf16[512,512]{1,0:T(8,128)(2,1)} %occ_dens.1, bf16[512,512]{1,0:T(8,128)(2,1)} %virt_dens.1), custom_call_target="tpu_custom_call" | custom-call | tf_op jit(solution)/shard_map/pallas_call | solution.py:320
  75.7 1.9 %copy.16 = f32[1,256,512]{2,1,0:T(8,128)} copy(f32[1,256,512]{2,1,0:T(8,128)} %bitcast.11) | data formatting | bytes 1048576
  77.5 1.7 %copy.17 = f32[256,256]{1,0:T(8,128)} copy(f32[256,256]{1,0:T(8,128)} %get-tuple-element.9) | data formatting | bytes 524288
  (1 shorter events, 0.0 us)

commit v3 on v2

--- a/solution.py
+++ b/solution.py
@@ -210,7 +210,7 @@
 
             pair_out[:, g * cols_group:(g + 1) * cols_group] = summed(g, 0)
 
-    ahead = 2
+    ahead = min(4, pieces)
     ready = 0
     closed = 0
 
@@ -221,12 +221,22 @@
     own(0)
     own(1)
     lax.fori_loop(0, batch, one_occ, 0)
-    for c in range(min(ahead, pieces)):
+    total = None
+    for l in range(batch):
+        term = product(l, masked[l, pl.ds(r * self_cols, self_cols), :])
+        total = term if total is None else total + term
+    self_tile[...] = total * factor
+    for c in range(ahead):
+        if c + 2 < pieces:
+            own(c + 2)
         relay(c)
         end_occ(c)
+        if c == 0:
+            for j in range(1, orbs):
+                self_copy(j).start()
     for c in range(pieces):
-        if c + 2 < pieces:
-            own(c + 2)
+        if c + ahead + 2 < pieces:
+            own(c + ahead + 2)
         if c + ahead < pieces:
             relay(c + ahead)
             end_occ(c + ahead)
@@ -235,15 +245,6 @@
             group(ready)
             ready += 1
         complete(c)
-        if c == 0:
-            total = None
-            for l in range(batch):
-                term = product(l, masked[l, pl.ds(r * self_cols, self_cols), :])
-                total = term if total is None else total + term
-            self_tile[...] = total * factor
-        if c == 1:
-            for j in range(1, orbs):
-                self_copy(j).start()
         if filled and c == pieces - 2 and closed + 1 < ready:
             finish(closed)
             closed += 1
@@ -310,9 +311,8 @@
     half = batch // reps
     rows_out = aux_rows // orbs
     self_cols = aux_rows // reps
-    weights = block_mask.astype(jnp.bfloat16)
-    spread = jnp.repeat(jnp.repeat(weights, BLOCK, axis=0), BLOCK, axis=1)
-    masked = jnp.transpose(slab, (1, 0, 2)) * spread[None]
+    spread = jnp.repeat(jnp.repeat(block_mask, BLOCK, axis=0), BLOCK, axis=1)
+    masked = jnp.transpose(slab, (1, 0, 2)) * spread.astype(jnp.bfloat16)[None]
     factor = 1.0 / math.sqrt(batch * orb_cols * orbs)
     dma = pltpu.SemaphoreType.DMA
     vmem = pl.BlockSpec(memory_space=pltpu.VMEM)

time: 79.5 us -> 80.6 us (1.014)
  Pallas kernels: 69.9 us -> 71.1 us
    pallas_call x1, Pallas kernels: 69.9 us -> 71.1 us  [per_device(): pl.pallas_call(functools.partial(kernel, (chips, orbs, reps, pieces, grou...]
where the time goes in v3:
time: 80.6 us; the launch traced here: 80.3 us
  Pallas kernels  71.1 us (88%)
  other arithmetic  4.36 us (5%)
  local copies, waits for them, and re-layouts  4.24 us (5%)
    pallas_call x1, Pallas kernels, per_device(): pl.pallas_call(functools.partial(kernel, (chips, orbs, reps, pieces, grou...  71.1 us
    mul x1, other arithmetic, per_device(): masked = jnp.transpose(slab, (1, 0, 2)) * spread.astype(jnp.bfloat16)[None]  3.67 us
    unnamed x3, local copies, waits for them, and re-layouts  3.62 us

profile of v3, /device:TPU:0, one launch (start us, length us, event | category | flops | bytes accessed | tf_op | source)
XLA Modules:
  0.0 80.3 jit_solution(16600549267062367988)
XLA Ops:
  0.6 0.7 convert_element_type.15
  1.3 0.6 broadcast_in_dim.11
  1.9 0.1 copy.13
  2.0 3.7 %fusion.masked = bf16[4,512,512]{2,1,0:T(8,128)(2,1)} fusion(bf16[512,4,512]{2,1,0:T(4,128)(2,1)} %param.5, bf16[512,512]{1,0:T(8,128)(2,1)S(1)} %bitcast.8), kind=kLoop, calls=%fused_computation.1 | loop fusion | flops 1048576 | bytes 4718592 | tf_op jit(solution)/shard_map/mul | solution.py:315
  5.7 71.1 %shard_map.68 = (f32[256,512]{1,0:T(8,128)}, f32[256,256]{1,0:T(8,128)}) custom-call(s32[2,8]{1,0:T(2,128)} %match_ref.1, bf16[4,512,512]{2,1,0:T(8,128)(2,1)} %fusion.masked, bf16[512,512]{1,0:T(8,128)(2,1)} %occ_dens.1, bf16[512,512]{1,0:T(8,128)(2,1)} %virt_dens.1), custom_call_target="tpu_custom_call" | custom-call | tf_op jit(solution)/shard_map/pallas_call | solution.py:320
  76.8 1.9 %copy.16 = f32[1,256,512]{2,1,0:T(8,128)} copy(f32[1,256,512]{2,1,0:T(8,128)} %bitcast.11) | data formatting | bytes 1048576
  78.7 1.7 %copy.17 = f32[256,256]{1,0:T(8,128)} copy(f32[256,256]{1,0:T(8,128)} %get-tuple-element.9) | data formatting | bytes 524288
  (1 shorter events, 0.0 us)

commit v4 on v2

--- a/solution.py
+++ b/solution.py
@@ -210,7 +210,7 @@
 
             pair_out[:, g * cols_group:(g + 1) * cols_group] = summed(g, 0)
 
-    ahead = 2
+    ahead = min(3, pieces)
     ready = 0
     closed = 0
 

time: 79.5 us -> 79.2 us (level)
  no operation moved by 1% of the time
where the time goes in v4:
time: 79.2 us; the launch traced here: 78.9 us
  Pallas kernels  69.7 us (88%)
  other arithmetic  4.36 us (6%)
  local copies, waits for them, and re-layouts  4.24 us (5%)
    pallas_call x1, Pallas kernels, per_device(): pl.pallas_call(functools.partial(kernel, (chips, orbs, reps, pieces, grou...  69.7 us
    mul x1, other arithmetic, per_device(): masked = jnp.transpose(slab, (1, 0, 2)) * spread[None]  3.67 us
    unnamed x3, local copies, waits for them, and re-layouts  3.62 us

profile of v4, /device:TPU:0, one launch (start us, length us, event | category | flops | bytes accessed | tf_op | source)
XLA Modules:
  0.0 78.9 jit_solution(5884213782103787817)
XLA Ops:
  0.6 0.7 convert_element_type.3
  1.3 0.6 broadcast_in_dim.10
  1.9 0.1 copy.13
  2.0 3.7 %fusion.masked = bf16[4,512,512]{2,1,0:T(8,128)(2,1)} fusion(bf16[512,4,512]{2,1,0:T(4,128)(2,1)} %param.5, bf16[512,512]{1,0:T(8,128)(2,1)S(1)} %bitcast.8), kind=kLoop, calls=%fused_computation.1 | loop fusion | flops 1048576 | bytes 4718592 | tf_op jit(solution)/shard_map/mul | solution.py:315
  5.7 69.7 %shard_map.68 = (f32[256,512]{1,0:T(8,128)}, f32[256,256]{1,0:T(8,128)}) custom-call(s32[2,8]{1,0:T(2,128)} %match_ref.1, bf16[4,512,512]{2,1,0:T(8,128)(2,1)} %fusion.masked, bf16[512,512]{1,0:T(8,128)(2,1)} %occ_dens.1, bf16[512,512]{1,0:T(8,128)(2,1)} %virt_dens.1), custom_call_target="tpu_custom_call" | custom-call | tf_op jit(solution)/shard_map/pallas_call | solution.py:320
  75.4 1.9 %copy.16 = f32[1,256,512]{2,1,0:T(8,128)} copy(f32[1,256,512]{2,1,0:T(8,128)} %bitcast.11) | data formatting | bytes 1048576
  77.2 1.7 %copy.17 = f32[256,256]{1,0:T(8,128)} copy(f32[256,256]{1,0:T(8,128)} %get-tuple-element.9) | data formatting | bytes 524288
  (1 shorter events, 0.0 us)
